TPU v7x, 32 devices: a whole 2x2x4 slice. The times are simulated.
32 devices in a mesh: orb: 8 (over z, x), slab: 4 (over y, core).
Axes of the slice: x: 2, y: 2, z: 4, core: 2. Of those that a mesh axis runs over, the one named last changes fastest.
Arguments:
- orbitals: bfloat16 [8, 64, 64, 128], P('orb', 'slab'), may hold values from -6 to 6
- pair_table: int32 [64, 3], P('orb'), may hold values from -1 to 7, as said below
Outputs:
- exchange_action: float32 [8, 64, 64, 128], P('orb', 'slab')
Inputs may be any that keep to these rules, and one draw needn't show every extreme that they name: `pair_table`: A live slot holds (m, n, s) with m <= n and s in 0, 1; an empty slot holds -1 in all three columns. A block of 8 slots has its live slots first. No (m, n, s) appears twice in the table. Exactly 36 slots are live, and the 8 blocks hold, in some order, k * 1 live slots for k = 1 to 8.
All inputs are finite; a program needn't handle non-finite values.
Results may differ from a plain program's by a relative error of at most 0.0003.
Values may be sent and summed in bfloat16 or wider, within the bound.
A program may use at most 64 MiB of HBM per device.

v0:
```python
import functools
import math

import jax
import jax.numpy as jnp
import numpy as np
from jax import lax
from jax.experimental import pallas as pl
from jax.experimental.pallas import tpu as pltpu
from jax.sharding import PartitionSpec as P

exchange_fraction = 0.25
cell_ratio = 8.0
MESH = pl.DeviceIdType.MESH
VMEM_SPEC = pl.BlockSpec(memory_space=pltpu.VMEM)
ANY_SPEC = pl.BlockSpec(memory_space=pl.ANY)


def folded(values, grid_len):
    return jnp.minimum(values, grid_len - values).astype(jnp.float32)


def hartley(grid_len):
    rows_idx = np.arange(grid_len)
    angles = 2.0 * math.pi / grid_len * (rows_idx[:, None] * rows_idx[None, :] % grid_len)
    return ((np.cos(angles) + np.sin(angles)) / math.sqrt(grid_len)).astype(np.float32)


def split_const(values):
    high = values.astype(jnp.bfloat16)
    return high, (values - high.astype(np.float32)).astype(jnp.bfloat16)


def split(values):
    high = values.astype(jnp.bfloat16)
    low = (values - high.astype(jnp.float32)).astype(jnp.bfloat16)
    return high, low


def coulomb(grid_len, slab_len, slab_index):
    planes_x = cell_ratio * folded(jnp.arange(grid_len, dtype=jnp.int32), grid_len)
    rows_y = folded(slab_index * slab_len + jnp.arange(slab_len, dtype=jnp.int32), grid_len)
    depth_z = folded(jnp.arange(2 * grid_len, dtype=jnp.int32) % grid_len, grid_len)
    scale_k = 2.0 * math.pi / grid_len * (2.0 * math.pi / grid_len)
    squared = scale_k * (
        planes_x[:, None, None] * planes_x[:, None, None]
        + rows_y[None, :, None] * rows_y[None, :, None]
        + depth_z[None, None, :] * depth_z[None, None, :]
    )
    safe_sq = jnp.where(squared > 0, squared, 1.0)
    return jnp.where(squared > 0, -exchange_fraction / safe_sq, 0.0)


def axis_parts(count):
    inner = 1
    while inner * inner * 4 <= count and count % (inner * 2) == 0:
        inner *= 2
    return count // inner, inner


def peer(index):
    return {"orb": index}


def greet_all(count, me):
    barrier = pltpu.get_barrier_semaphore()
    for step in range(1, count):
        pl.semaphore_signal(
            barrier, inc=1, device_id=peer(lax.rem(me + step, count)), device_id_type=MESH
        )
    pl.semaphore_wait(barrier, count - 1)


def gather_kernel(count, own_ref, table_ref, out_ref, tables_ref, local_sem, up_send, up_recv,
                  down_send, down_recv, side_send, side_recv, tab_send, tab_recv):
    outer, inner = axis_parts(count)
    me = lax.axis_index("orb")
    z_pos, x_pos = me // inner, me % inner
    greet_all(count, me)

    def slot(z_at, x_at):
        return out_ref.at[z_at * inner + x_at]

    def up_copy(step, src):
        return pltpu.make_async_remote_copy(
            src_ref=src, dst_ref=slot(z_pos - step, x_pos), send_sem=up_send.at[step],
            recv_sem=up_recv.at[step], device_id=peer((z_pos + 1) * inner + x_pos),
            device_id_type=MESH)

    def down_copy(step, src):
        return pltpu.make_async_remote_copy(
            src_ref=src, dst_ref=slot(z_pos + step, x_pos), send_sem=down_send.at[step],
            recv_sem=down_recv.at[step], device_id=peer((z_pos - 1) * inner + x_pos),
            device_id_type=MESH)

    def side_copy(hop, z_at, src):
        return pltpu.make_async_remote_copy(
            src_ref=src, dst_ref=slot(z_at, x_pos), send_sem=side_send.at[hop - 1, z_at],
            recv_sem=side_recv.at[hop - 1, z_at],
            device_id=peer(z_pos * inner + lax.rem(x_pos + hop, inner)), device_id_type=MESH)

    def tab_copy(step):
        return pltpu.make_async_remote_copy(
            src_ref=table_ref, dst_ref=tables_ref.at[me], send_sem=tab_send.at[step - 1],
            recv_sem=tab_recv.at[step - 1], device_id=peer(lax.rem(me + step, count)),
            device_id_type=MESH)

    has_up, has_down = z_pos + 1 < outer, z_pos >= 1

    @pl.when(has_up)
    def _():
        up_copy(0, own_ref).start()

    @pl.when(has_down)
    def _():
        down_copy(0, own_ref).start()

    for hop in range(1, inner):
        side_copy(hop, z_pos, own_ref).start()
    for step in range(1, count):
        tab_copy(step).start()
    keep = pltpu.make_async_copy(own_ref, out_ref.at[me], local_sem.at[0])
    keep.start()
    keep_tab = pltpu.make_async_copy(table_ref, tables_ref.at[me], local_sem.at[1])
    keep_tab.start()

    for step in range(1, outer):
        @pl.when(z_pos - step >= 0)
        def _():
            held = slot(z_pos - step, x_pos)
            up_copy(step - 1, held).wait_recv()

            @pl.when(has_up)
            def _():
                up_copy(step, held).start()

            for hop in range(1, inner):
                side_copy(hop, z_pos - step, held).start()

        @pl.when(z_pos + step < outer)
        def _():
            held = slot(z_pos + step, x_pos)
            down_copy(step - 1, held).wait_recv()

            @pl.when(has_down)
            def _():
                down_copy(step, held).start()

            for hop in range(1, inner):
                side_copy(hop, z_pos + step, held).start()

    keep.wait()
    keep_tab.wait()
    for hop in range(1, inner):
        for z_at in range(outer):
            side_copy(hop, z_at, own_ref).wait_recv()
            side_copy(hop, z_at, own_ref).wait_send()
    for step in range(1, count):
        tab_copy(step).wait_recv()
        tab_copy(step).wait_send()
    for step in range(outer):
        @pl.when(has_up & (z_pos - step >= 0))
        def _():
            up_copy(step, own_ref).wait_send()

        @pl.when(has_down & (z_pos + step < outer))
        def _():
            down_copy(step, own_ref).wait_send()


def gather_all(own, table, count):
    outer, inner = axis_parts(count)
    dma = pltpu.SemaphoreType.DMA
    return pl.pallas_call(
        functools.partial(gather_kernel, count),
        out_shape=(
            jax.ShapeDtypeStruct((count,) + own.shape, own.dtype),
            jax.ShapeDtypeStruct((count,) + table.shape, table.dtype),
        ),
        in_specs=[VMEM_SPEC, VMEM_SPEC],
        out_specs=(ANY_SPEC, ANY_SPEC),
        scratch_shapes=[dma((2,)), dma((outer,)), dma((outer,)), dma((outer,)), dma((outer,)),
                        dma((max(inner - 1, 1), outer)), dma((max(inner - 1, 1), outer)),
                        dma((count - 1,)), dma((count - 1,))],
        compiler_params=pltpu.CompilerParams(collective_id=0, has_side_effects=True),
    )(own, table)


def scatter_kernel(count, parts_ref, out_ref, side_in, line_in, sums, own_sem, side_send,
                   side_recv, line_send, line_recv):
    outer, inner = axis_parts(count)
    me = lax.axis_index("orb")
    z_pos, x_pos = me // inner, me % inner
    greet_all(count, me)

    def side_copy(hop, turn):
        z_at = lax.rem(z_pos + turn, outer)
        x_to = lax.rem(x_pos + hop, inner)
        return pltpu.make_async_remote_copy(
            src_ref=parts_ref.at[z_at * inner + x_to], dst_ref=side_in.at[hop - 1, turn],
            send_sem=side_send.at[hop - 1, turn], recv_sem=side_recv.at[hop - 1, turn],
            device_id=peer(z_pos * inner + x_to), device_id_type=MESH)

    def line_copy(turn):
        z_at = lax.rem(z_pos + turn, outer)
        return pltpu.make_async_remote_copy(
            src_ref=sums.at[turn], dst_ref=line_in.at[turn - 1],
            send_sem=line_send.at[turn - 1], recv_sem=line_recv.at[turn - 1],
            device_id=peer(z_at * inner + x_pos), device_id_type=MESH)

    def own_copy(turn):
        z_at = lax.rem(z_pos + turn, outer)
        return pltpu.make_async_copy(
            parts_ref.at[z_at * inner + x_pos], sums.at[turn], own_sem.at[turn])

    order = list(range(1, outer)) + [0]
    for turn in order:
        for hop in range(1, inner):
            side_copy(hop, turn).start()
        own_copy(turn).start()
    for turn in order:
        own_copy(turn).wait()
        for hop in range(1, inner):
            side_copy(hop, turn).wait_recv()
            sums[turn] = sums[turn] + side_in[hop - 1, turn]
        if turn:
            line_copy(turn).start()
    total = sums[0]
    for turn in range(1, outer):
        line_copy(turn).wait_recv()
        total = total + line_in[turn - 1]
    out_ref[...] = total
    for turn in range(outer):
        for hop in range(1, inner):
            side_copy(hop, turn).wait_send()
        if turn:
            line_copy(turn).wait_send()


def scatter_sum(parts, count):
    outer, inner = axis_parts(count)
    dma = pltpu.SemaphoreType.DMA
    block = parts.shape[1:]
    sides, lines = max(inner - 1, 1), max(outer - 1, 1)
    return pl.pallas_call(
        functools.partial(scatter_kernel, count),
        out_shape=jax.ShapeDtypeStruct(block, parts.dtype),
        in_specs=[ANY_SPEC],
        out_specs=VMEM_SPEC,
        scratch_shapes=[
            pltpu.VMEM((sides, outer) + block, parts.dtype),
            pltpu.VMEM((lines,) + block, parts.dtype),
            pltpu.VMEM((outer,) + block, parts.dtype),
            dma((outer,)), dma((sides, outer)), dma((sides, outer)), dma((lines,)), dma((lines,)),
        ],
        compiler_params=pltpu.CompilerParams(collective_id=1, has_side_effects=True),
    )(parts)


def depth_turn(rows, depth_ref):
    width = rows.shape[1]
    high, low = split(rows)
    both = jnp.dot(jnp.concatenate([high, low], axis=1), depth_ref[...],
                   preferred_element_type=jnp.float32)
    return both[:, :width] + both[:, width:]


def pair_turn(first, second, left_ref):
    high, low = split(jnp.concatenate([first, second], axis=1))
    return jnp.dot(left_ref[...], jnp.concatenate([high, low, high], axis=0),
                   preferred_element_type=jnp.float32)


def forward_kernel(grid_len, ids_ref, left_ref, right_ref, depth_ref, turn_ref, out_ref):
    step = pl.program_id(0)
    left = left_ref[0].astype(jnp.float32)
    right = right_ref[0].astype(jnp.float32)
    width = right.shape[1]
    partner = jnp.where(ids_ref[step, 2] == 1, pltpu.roll(right, grid_len, 1), right)
    density = jnp.where(ids_ref[step, 3] == 1, left * partner, 0.0)
    flat = depth_turn(density, depth_ref)
    for x_at in range(0, flat.shape[0] // grid_len, 2):
        low, mid, high = x_at * grid_len, (x_at + 1) * grid_len, (x_at + 2) * grid_len
        done = pair_turn(flat[low:mid], flat[mid:high], turn_ref)
        out_ref[0, low:mid] = done[:, :width]
        out_ref[0, mid:high] = done[:, width:]


def middle_kernel(grid_len, slab_len, in_ref, kernel_ref, turn_ref, out_ref):
    width = in_ref.shape[2]
    for row in range(0, slab_len, 2):
        one = pl.ds(row, grid_len, stride=slab_len)
        two = pl.ds(row + 1, grid_len, stride=slab_len)
        done = pair_turn(in_ref[0, one, :], in_ref[0, two, :], turn_ref)
        back = pair_turn(done[:, :width] * kernel_ref[one, :], done[:, width:] * kernel_ref[two, :],
                         turn_ref)
        out_ref[0, one, :] = back[:, :width]
        out_ref[0, two, :] = back[:, width:]


def backward_kernel(grid_len, ids_ref, in_ref, left_ref, right_ref, depth_ref, turn_ref, out_ref,
                    flat_ref):
    step = pl.program_id(0)

    @pl.when(step == 0)
    def _():
        out_ref[...] = jnp.zeros_like(out_ref)

    width = flat_ref.shape[1]
    for x_at in range(0, flat_ref.shape[0] // grid_len, 2):
        low, mid, high = x_at * grid_len, (x_at + 1) * grid_len, (x_at + 2) * grid_len
        done = pair_turn(in_ref[0, low:mid], in_ref[0, mid:high], turn_ref)
        flat_ref[low:mid] = done[:, :width]
        flat_ref[mid:high] = done[:, width:]
    potential = depth_turn(flat_ref[...], depth_ref)
    first_id, second_id = ids_ref[step, 0], ids_ref[step, 1]
    flipped = ids_ref[step, 2] == 1
    is_used = ids_ref[step, 3] == 1

    @pl.when(is_used)
    def _():
        right = right_ref[0].astype(jnp.float32)
        partner = jnp.where(flipped, pltpu.roll(right, grid_len, 1), right)
        out_ref[first_id] += potential * partner

    @pl.when(is_used & (first_id != second_id))
    def _():
        second = potential * left_ref[0].astype(jnp.float32)
        out_ref[second_id] += jnp.where(flipped, pltpu.roll(second, grid_len, 1), second)


def local(orbitals, pair_table, n_orb):
    couples_own, slab_len, grid_len, width = orbitals.shape
    rows = slab_len * grid_len
    capacity = pair_table.shape[0]
    couples = couples_own * n_orb
    padded = jnp.pad(pair_table, ((0, 0), (0, 128 - pair_table.shape[1])), constant_values=-1)
    gathered, tables = gather_all(orbitals.reshape(couples_own * rows, width), padded, n_orb)
    gathered = gathered.reshape(couples, rows, width)
    table = tables.reshape(n_orb * capacity, 128)[:, :3]

    live_total = sum(capacity * (k + 1) // n_orb for k in range(n_orb))
    per_device = -(-live_total // n_orb)
    is_live = table[:, 0] >= 0
    rank = jnp.cumsum(is_live.astype(jnp.int32)) - 1
    wanted = jnp.arange(per_device, dtype=jnp.int32) * n_orb + lax.axis_index("orb")
    hits = (rank[None, :] == wanted[:, None]) & is_live[None, :]
    picked = jnp.sum(jnp.where(hits[:, :, None], table[None], 0), axis=1)
    used = jnp.any(hits, axis=1).astype(jnp.int32)
    ids = jnp.concatenate([picked, used[:, None]], axis=1)

    mat = hartley(grid_len)
    mat_high, mat_low = split_const(mat)
    turn_mat = jnp.asarray(np.concatenate([mat_high, mat_high, mat_low], axis=1))
    deep_high, deep_low = split_const(np.kron(np.eye(2, dtype=np.float32), mat))
    depth_mat = jnp.asarray(np.block([[deep_high, deep_low],
                                      [deep_high, np.zeros_like(deep_low)]]))
    kernel = coulomb(grid_len, slab_len, lax.axis_index("slab")).reshape(grid_len * slab_len, width)

    def whole(shape):
        return pl.BlockSpec(shape, lambda j, *ids: (0,) * len(shape))

    left_spec = pl.BlockSpec((1, rows, width), lambda j, ids: (ids[j, 0], 0, 0))
    right_spec = pl.BlockSpec((1, rows, width), lambda j, ids: (ids[j, 1], 0, 0))
    slot_spec = pl.BlockSpec((1, rows, width), lambda j, *ids: (j, 0, 0))
    slots_shape = jax.ShapeDtypeStruct((per_device, rows, width), jnp.float32)

    spectra = pl.pallas_call(
        functools.partial(forward_kernel, grid_len),
        out_shape=slots_shape,
        grid_spec=pltpu.PrefetchScalarGridSpec(
            num_scalar_prefetch=1, grid=(per_device,),
            in_specs=[left_spec, right_spec, whole(depth_mat.shape), whole(turn_mat.shape)],
            out_specs=slot_spec),
    )(ids, gathered, gathered, depth_mat, turn_mat)
    crossed = lax.all_to_all(spectra.reshape(per_device, slab_len, grid_len, width), "slab",
                             split_axis=2, concat_axis=1, tiled=True)
    solved = pl.pallas_call(
        functools.partial(middle_kernel, grid_len, slab_len),
        out_shape=slots_shape,
        grid=(per_device,),
        in_specs=[slot_spec, whole(kernel.shape), whole(turn_mat.shape)],
        out_specs=slot_spec,
    )(crossed.reshape(per_device, rows, width), kernel, turn_mat)
    returned = lax.all_to_all(solved.reshape(per_device, grid_len, slab_len, width), "slab",
                              split_axis=1, concat_axis=2, tiled=True)
    totals = pl.pallas_call(
        functools.partial(backward_kernel, grid_len),
        out_shape=jax.ShapeDtypeStruct((couples, rows, width), jnp.float32),
        grid_spec=pltpu.PrefetchScalarGridSpec(
            num_scalar_prefetch=1, grid=(per_device,),
            in_specs=[slot_spec, left_spec, right_spec, whole(depth_mat.shape),
                      whole(turn_mat.shape)],
            out_specs=whole((couples, rows, width)),
            scratch_shapes=[pltpu.VMEM((rows, width), jnp.float32)]),
    )(ids, returned.reshape(per_device, rows, width), gathered, gathered, depth_mat, turn_mat)

    own = scatter_sum(totals.reshape(n_orb, couples_own * rows, width), n_orb)
    own = own.reshape(couples_own, rows, width)
    cell_count = grid_len * grid_len * grid_len

    def swap(values):
        return jnp.concatenate([values[..., grid_len:], values[..., :grid_len]], axis=-1)

    def lanes(values):
        summed = values.reshape(values.shape[:-1] + (2, grid_len)).sum(axis=-1)
        return jnp.repeat(summed, grid_len, axis=-1)

    basis = gathered.astype(jnp.float32)
    turned = swap(own)
    straight = jnp.sum(basis[None] * own[:, None], axis=2)
    across = jnp.sum(basis[None] * turned[:, None], axis=2)
    both = lax.psum(lanes(jnp.stack([straight, across])) / cell_count, "slab")
    kept = jnp.sum(both[0][:, :, None, :] * basis[None], axis=1)
    moved = jnp.sum(both[1][:, :, None, :] * basis[None], axis=1)
    return (own - kept - swap(moved)).reshape(orbitals.shape)


def solution(mesh):
    placed = (P("orb", "slab", None, None), P("orb", None))
    return jax.shard_map(
        functools.partial(local, n_orb=mesh.shape["orb"]),
        mesh=mesh, in_specs=placed, out_specs=P("orb", "slab", None, None), check_vma=False
    )
```

profile of v0, /device:TPU:0, one launch (start us, length us, event | category | flops | bytes accessed | tf_op | source)
XLA Modules:
  0.0 211.2 jit_solution(17429114716284629580)
XLA Ops:
  0.0 0.8 copy.37
  0.8 0.6 pad.4.table_ref
  1.4 32.4 %shard_map.46 = (bf16[8,1024,128]{2,1,0:T(8,128)(2,1)}, s32[8,8,128]{2,1,0:T(8,128)}) custom-call(bf16[1024,128]{1,0:T(8,128)(2,1)} %bitcast.41, s32[8,128]{1,0:T(8,128)} %pad.4.table_ref), custom_call_target="tpu_custom_call" | custom-call | tf_op jit(solution)/shard_map/pallas_call | solution.py:174
  33.7 0.8 copy.53
  34.6 0.8 copy.40
  35.4 0.1 copy.39
  35.5 0.1 reduce-window.8
  35.6 0.1 add_reduce_fusion
  35.7 0.2 fusion.12
  35.9 0.1 copy.41
  36.0 0.2 select_reduce_fusion
  36.2 0.7 pad_add_fusion.ids_ref
  36.9 7.0 %shard_map.47 = f32[5,1024,128]{2,1,0:T(8,128)} custom-call(s32[5,4]{1,0:T(8,128)} %pad_add_fusion.ids_ref, bf16[8,1024,128]{2,1,0:T(8,128)(2,1)} %get-tuple-element.8.left_ref.right_ref, bf16[8,1024,128]{2,1,0:T(8,128)(2,1)} %get-tuple-element.8.left_ref.right_ref, bf16[256,256]{1,0:T(8,128)(2,1)} %constant.62.clone.depth_ref, ...), custom_call_target="tpu_custom_call" | custom-call | tf_op jit(solution)/shard_map/pallas_call | solution.py:368
  43.8 4.8 %copy.42 = f32[5,16,64,128]{3,1,0,2:T(8,128)} copy(f32[5,16,64,128]{3,2,1,0:T(8,128)} %bitcast.39) | data formatting | bytes 5242880 | tf_op jit(solution)/shard_map/reshape | solution.py:376
  48.6 3.7 %all-to-all-start = ((f32[5,16,64,128]{3,1,0,2:T(8,128)}), f32[5,16,64,128]{3,1,0,2:T(8,128)S(1)}, u32[]{:S(2)}, u32[]{:S(2)}) async-start(f32[5,16,64,128]{3,1,0,2:T(8,128)} %copy.42), calls=%async_computation | async-start | bytes 5242880 | tf_op jit(solution)/shard_map/all_to_all | solution.py:376
  52.3 0.1 add.78
  52.4 0.1 add.79
  52.5 0.1 add.83
  52.6 1.0 compare_select_fusion.kernel_ref
  53.6 30.0 %all-to-all-done = f32[5,16,64,128]{3,1,0,2:T(8,128)S(1)} async-done(((f32[5,16,64,128]{3,1,0,2:T(8,128)}), f32[5,16,64,128]{3,1,0,2:T(8,128)S(1)}, u32[]{:S(2)}, u32[]{:S(2)}) %all-to-all-start) | async-done | bytes 2621472 | tf_op jit(solution)/shard_map/all_to_all | solution.py:376
  83.5 2.4 %copy.44 = f32[5,4,16,16,128]{4,3,2,1,0:T(8,128)} copy(f32[5,4,16,16,128]{4,2,0,3,1:T(8,128)S(1)} %bitcast.35) | data formatting | bytes 5242880 | tf_op jit(solution)/shard_map/all_to_all | solution.py:376
  86.0 6.2 %shard_map.48 = f32[5,1024,128]{2,1,0:T(8,128)} custom-call(f32[5,1024,128]{2,1,0:T(8,128)} %bitcast.36, f32[1024,128]{1,0:T(8,128)} %compare_select_fusion.kernel_ref, bf16[64,192]{1,0:T(8,128)(2,1)} %constant.61.clone.turn_ref), custom_call_target="tpu_custom_call" | custom-call | tf_op jit(solution)/shard_map/pallas_call | solution.py:378
  92.2 1.9 copy.45
  94.1 33.8 %all_to_all.30 = f32[5,64,16,128]{3,2,0,1:T(8,128)S(1)} all-to-all(f32[5,64,16,128]{3,2,0,1:T(8,128)S(1)} %copy.45), channel_id=1, replica_groups=mesh['orb'=8,'slab'=4] {'slab'}, dimensions={1} | all-to-all | bytes 5242880 | tf_op jit(solution)/shard_map/all_to_all | solution.py:385
  127.9 1.9 copy.47
  129.8 9.1 %shard_map.49.parts_ref = f32[8,1024,128]{2,1,0:T(8,128)} custom-call(s32[5,4]{1,0:T(8,128)} %pad_add_fusion.ids_ref, f32[5,1024,128]{2,1,0:T(8,128)} %bitcast.34, bf16[8,1024,128]{2,1,0:T(8,128)(2,1)} %get-tuple-element.8.left_ref.right_ref, bf16[8,1024,128]{2,1,0:T(8,128)(2,1)} %get-tuple-element.8.left_ref.right_ref, ...), custom_call_target="tpu_custom_call" | custom-call | tf_op jit(solution)/shard_map/pallas_call | solution.py:387
  139.0 0.0 copy-start
  139.0 60.6 %shard_map.50 = f32[1024,128]{1,0:T(8,128)} custom-call(f32[8,1024,128]{2,1,0:T(8,128)} %shard_map.49.parts_ref), custom_call_target="tpu_custom_call" | custom-call | tf_op jit(solution)/shard_map/pallas_call | solution.py:245
  199.5 1.4 fusion.13
  200.9 0.2 maximum_bitcast_fusion
  201.2 0.0 copy-done
  201.2 0.0 copy-start.1
  201.2 1.8 fusion
  203.0 0.1 stack.9
  203.1 0.1 stack.10
  203.1 0.1 maximum_reduce_fusion
  203.3 0.1 broadcast_in_dim.31
  203.3 0.1 div.19
  203.4 5.7 %psum.7 = f32[2,1,8,128]{3,2,1,0:T(8,128)S(1)} all-reduce(f32[2,1,8,128]{3,2,1,0:T(8,128)S(1)} %div.19), channel_id=1, replica_groups=mesh['orb'=8,'slab'=4] {'slab'}, use_global_device_ids=true, to_apply=%region_6.7 | all-reduce | flops 2048 | bytes 16384 | tf_op jit(solution)/shard_map/psum | solution.py:413
  209.2 0.7 fusion.2
  209.9 0.2 slice_bitcast_fusion.1
  210.1 0.0 copy-done.1
  210.1 1.0 maximum_subtract_fusion
  (10 shorter events, 0.1 us)
Async XLA Ops:
  48.6 34.9 %all-to-all-start = ((f32[5,16,64,128]{3,1,0,2:T(8,128)}), f32[5,16,64,128]{3,1,0,2:T(8,128)S(1)}, u32[]{:S(2)}, u32[]{:S(2)}) async-start(f32[5,16,64,128]{3,1,0,2:T(8,128)} %copy.42), calls=%async_computation | async-start | bytes 5242880 | tf_op jit(solution)/shard_map/all_to_all | solution.py:376
  139.0 62.2 %copy-start = (bf16[8,1024,128]{2,1,0:T(8,128)(2,1)S(1)}, bf16[8,1024,128]{2,1,0:T(8,128)(2,1)}, u32[]{:S(2)}) copy-start(bf16[8,1024,128]{2,1,0:T(8,128)(2,1)} %get-tuple-element.8.left_ref.right_ref) | copy-start | bytes 6291460
  201.2 9.0 %copy-start.1 = (f32[1024,128]{1,0:T(8,128)S(1)}, f32[1024,128]{1,0:T(8,128)}, u32[]{:S(2)}) copy-start(f32[1024,128]{1,0:T(8,128)} %shard_map.50) | copy-start | bytes 1572868
where the time goes:
time: 212 us; the launch traced here: 211 us
  Pallas kernels  115 us (54%)
  blocking collectives  39.5 us (19%)
  waiting for transfers between devices  30 us (14%)
  local copies, waits for them, and re-layouts  16.4 us (8%)
  other arithmetic  6.17 us (3%)
  starting transfers between devices  3.65 us (2%)
    pallas_call x1, Pallas kernels, scatter_sum(): pl.pallas_call(functools.partial(scatter_kernel, count), out_shape=jax.Sh...  60.6 us
    all_to_all x1, blocking collectives, local(): lax.all_to_all(solved.reshape(per_device, grid_len, slab_len, width), 'sl...  33.8 us
    pallas_call x1, Pallas kernels, gather_all(): pl.pallas_call(functools.partial(gather_kernel, count), out_shape=(jax.Sh...  32.4 us
    all_to_all x1, waiting for transfers between devices, local(): lax.all_to_all(spectra.reshape(per_device, slab_len, grid_len, width), 's...  30 us
    pallas_call x1, Pallas kernels, local(): pl.pallas_call(functools.partial(backward_kernel, grid_len), out_shape=ja...  9.13 us
    pallas_call x1, Pallas kernels, local(): pl.pallas_call(functools.partial(forward_kernel, grid_len), out_shape=slo...  6.98 us
    pallas_call x1, Pallas kernels, local(): pl.pallas_call(functools.partial(middle_kernel, grid_len, slab_len), out_...  6.25 us
    psum x1, blocking collectives, local(): both = lax.psum(lanes(jnp.stack([straight, across])) / cell_count, 'slab')  5.74 us
  transfers between devices with their start and end apart: 1, of which 1 were waited for; matrix products, arithmetic and copies ran while one was open for 1% of the time, Pallas kernels for 0%

commit v1 on v0

--- a/solution.py
+++ b/solution.py
@@ -186,77 +186,6 @@
     )(own, table)
 
 
-def scatter_kernel(count, parts_ref, out_ref, side_in, line_in, sums, own_sem, side_send,
-                   side_recv, line_send, line_recv):
-    outer, inner = axis_parts(count)
-    me = lax.axis_index("orb")
-    z_pos, x_pos = me // inner, me % inner
-    greet_all(count, me)
-
-    def side_copy(hop, turn):
-        z_at = lax.rem(z_pos + turn, outer)
-        x_to = lax.rem(x_pos + hop, inner)
-        return pltpu.make_async_remote_copy(
-            src_ref=parts_ref.at[z_at * inner + x_to], dst_ref=side_in.at[hop - 1, turn],
-            send_sem=side_send.at[hop - 1, turn], recv_sem=side_recv.at[hop - 1, turn],
-            device_id=peer(z_pos * inner + x_to), device_id_type=MESH)
-
-    def line_copy(turn):
-        z_at = lax.rem(z_pos + turn, outer)
-        return pltpu.make_async_remote_copy(
-            src_ref=sums.at[turn], dst_ref=line_in.at[turn - 1],
-            send_sem=line_send.at[turn - 1], recv_sem=line_recv.at[turn - 1],
-            device_id=peer(z_at * inner + x_pos), device_id_type=MESH)
-
-    def own_copy(turn):
-        z_at = lax.rem(z_pos + turn, outer)
-        return pltpu.make_async_copy(
-            parts_ref.at[z_at * inner + x_pos], sums.at[turn], own_sem.at[turn])
-
-    order = list(range(1, outer)) + [0]
-    for turn in order:
-        for hop in range(1, inner):
-            side_copy(hop, turn).start()
-        own_copy(turn).start()
-    for turn in order:
-        own_copy(turn).wait()
-        for hop in range(1, inner):
-            side_copy(hop, turn).wait_recv()
-            sums[turn] = sums[turn] + side_in[hop - 1, turn]
-        if turn:
-            line_copy(turn).start()
-    total = sums[0]
-    for turn in range(1, outer):
-        line_copy(turn).wait_recv()
-        total = total + line_in[turn - 1]
-    out_ref[...] = total
-    for turn in range(outer):
-        for hop in range(1, inner):
-            side_copy(hop, turn).wait_send()
-        if turn:
-            line_copy(turn).wait_send()
-
-
-def scatter_sum(parts, count):
-    outer, inner = axis_parts(count)
-    dma = pltpu.SemaphoreType.DMA
-    block = parts.shape[1:]
-    sides, lines = max(inner - 1, 1), max(outer - 1, 1)
-    return pl.pallas_call(
-        functools.partial(scatter_kernel, count),
-        out_shape=jax.ShapeDtypeStruct(block, parts.dtype),
-        in_specs=[ANY_SPEC],
-        out_specs=VMEM_SPEC,
-        scratch_shapes=[
-            pltpu.VMEM((sides, outer) + block, parts.dtype),
-            pltpu.VMEM((lines,) + block, parts.dtype),
-            pltpu.VMEM((outer,) + block, parts.dtype),
-            dma((outer,)), dma((sides, outer)), dma((sides, outer)), dma((lines,)), dma((lines,)),
-        ],
-        compiler_params=pltpu.CompilerParams(collective_id=1, has_side_effects=True),
-    )(parts)
-
-
 def depth_turn(rows, depth_ref):
     width = rows.shape[1]
     high, low = split(rows)
@@ -298,38 +227,164 @@
         out_ref[0, two, :] = back[:, width:]
 
 
-def backward_kernel(grid_len, ids_ref, in_ref, left_ref, right_ref, depth_ref, turn_ref, out_ref,
-                    flat_ref):
-    step = pl.program_id(0)
-
-    @pl.when(step == 0)
-    def _():
-        out_ref[...] = jnp.zeros_like(out_ref)
-
-    width = flat_ref.shape[1]
-    for x_at in range(0, flat_ref.shape[0] // grid_len, 2):
-        low, mid, high = x_at * grid_len, (x_at + 1) * grid_len, (x_at + 2) * grid_len
-        done = pair_turn(in_ref[0, low:mid], in_ref[0, mid:high], turn_ref)
-        flat_ref[low:mid] = done[:, :width]
-        flat_ref[mid:high] = done[:, width:]
-    potential = depth_turn(flat_ref[...], depth_ref)
-    first_id, second_id = ids_ref[step, 0], ids_ref[step, 1]
-    flipped = ids_ref[step, 2] == 1
-    is_used = ids_ref[step, 3] == 1
-
-    @pl.when(is_used)
-    def _():
-        right = right_ref[0].astype(jnp.float32)
-        partner = jnp.where(flipped, pltpu.roll(right, grid_len, 1), right)
-        out_ref[first_id] += potential * partner
-
-    @pl.when(is_used & (first_id != second_id))
-    def _():
-        second = potential * left_ref[0].astype(jnp.float32)
-        out_ref[second_id] += jnp.where(flipped, pltpu.roll(second, grid_len, 1), second)
-
-
-def local(orbitals, pair_table, n_orb):
+def return_kernel(n_orb, n_slab, chunks, couples_own, ids_ref, weights_ref, solved_ref, basis_ref,
+                  depth_ref, turn_ref, out_ref, back, terms, flat_ref, parts, side_in, line_in, sums,
+                  keep_sem, back_send, back_recv, side_send, side_recv, line_send, line_recv):
+    outer, inner = axis_parts(n_orb)
+    me, me_slab = lax.axis_index("orb"), lax.axis_index("slab")
+    z_pos, x_pos = me // inner, me % inner
+    slots, grid_len, slab_len, width = solved_ref.shape
+    planes = slab_len // chunks
+    rows = planes * grid_len
+
+    barrier = pltpu.get_barrier_semaphore()
+    for step in range(1, n_orb):
+        pl.semaphore_signal(barrier, inc=1, device_id=peer(lax.rem(me + step, n_orb)),
+                            device_id_type=MESH)
+    for step in range(1, n_slab):
+        pl.semaphore_signal(barrier, inc=1, device_id={"slab": lax.rem(me_slab + step, n_slab)},
+                            device_id_type=MESH)
+    pl.semaphore_wait(barrier, n_orb + n_slab - 2)
+
+    own_rows = pl.ds(pl.multiple_of(me_slab * slab_len, slab_len), slab_len)
+
+    def back_copy(chunk, hop):
+        to = lax.rem(me_slab + hop, n_slab)
+        return pltpu.make_async_remote_copy(
+            src_ref=solved_ref.at[:, pl.ds(to * slab_len + chunk * planes, planes)],
+            dst_ref=back.at[chunk, :, :, own_rows],
+            send_sem=back_send.at[chunk, hop - 1], recv_sem=back_recv.at[chunk, hop - 1],
+            device_id={"slab": to}, device_id_type=MESH)
+
+    def keep_copy(chunk):
+        return pltpu.make_async_copy(
+            solved_ref.at[:, pl.ds(me_slab * slab_len + chunk * planes, planes)],
+            back.at[chunk, :, :, own_rows], keep_sem.at[chunk])
+
+    def side_copy(chunk, hop, turn):
+        z_at = lax.rem(z_pos + turn, outer)
+        x_to = lax.rem(x_pos + hop, inner)
+        return pltpu.make_async_remote_copy(
+            src_ref=parts.at[chunk, z_at * inner + x_to], dst_ref=side_in.at[chunk, hop - 1, turn],
+            send_sem=side_send.at[chunk, hop - 1, turn], recv_sem=side_recv.at[chunk, hop - 1, turn],
+            device_id=peer(z_pos * inner + x_to), device_id_type=MESH)
+
+    def line_copy(chunk, turn):
+        z_at = lax.rem(z_pos + turn, outer)
+        return pltpu.make_async_remote_copy(
+            src_ref=sums.at[chunk, turn], dst_ref=line_in.at[chunk, turn - 1],
+            send_sem=line_send.at[chunk, turn - 1], recv_sem=line_recv.at[chunk, turn - 1],
+            device_id=peer(z_at * inner + x_pos), device_id_type=MESH)
+
+    order = list(range(1, outer)) + [0]
+
+    def compute(chunk):
+        keep_copy(chunk).wait()
+        for hop in range(1, n_slab):
+            back_copy(chunk, hop).wait_recv()
+
+        @pl.loop(0, slots)
+        def _(slot):
+            for x_at in range(0, planes, 2):
+                done = pair_turn(back[chunk, slot, x_at], back[chunk, slot, x_at + 1], turn_ref)
+                flat_ref[x_at * grid_len:(x_at + 1) * grid_len] = done[:, :width]
+                flat_ref[(x_at + 1) * grid_len:(x_at + 2) * grid_len] = done[:, width:]
+            potential = depth_turn(flat_ref[...], depth_ref)
+            flipped = ids_ref[slot, 2] == 1
+            span = pl.ds(chunk * rows, rows)
+            right = basis_ref[ids_ref[slot, 1], span].astype(jnp.float32)
+            left = basis_ref[ids_ref[slot, 0], span].astype(jnp.float32)
+            terms[2 * slot] = potential * jnp.where(flipped, pltpu.roll(right, grid_len, 1), right)
+            second = potential * left
+            terms[2 * slot + 1] = jnp.where(flipped, pltpu.roll(second, grid_len, 1), second)
+
+        tile = 32
+
+        @pl.loop(0, rows // tile)
+        def _(at):
+            here = pl.ds(pl.multiple_of(at * tile, tile), tile)
+
+            @pl.loop(0, n_orb)
+            def _(owner):
+                for k in range(couples_own):
+                    total = jnp.zeros((tile, width), jnp.float32)
+                    for term in range(2 * slots):
+                        total += weights_ref[owner * couples_own + k, term] * terms[term, here]
+                    parts[chunk, owner, k, here] = total
+
+        for turn in order:
+            for hop in range(1, inner):
+                side_copy(chunk, hop, turn).start()
+
+    def forward(chunk):
+        for turn in order:
+            merged = parts[chunk, lax.rem(z_pos + turn, outer) * inner + x_pos]
+            for hop in range(1, inner):
+                side_copy(chunk, hop, turn).wait_recv()
+                merged = merged + side_in[chunk, hop - 1, turn]
+            sums[chunk, turn] = merged
+            if turn:
+                line_copy(chunk, turn).start()
+
+    for chunk in range(chunks):
+        for hop in range(1, n_slab):
+            back_copy(chunk, hop).start()
+        keep_copy(chunk).start()
+    for chunk in range(chunks):
+        compute(chunk)
+        if chunk:
+            forward(chunk - 1)
+    forward(chunks - 1)
+    for chunk in range(chunks):
+        total = sums[chunk, 0]
+        for turn in range(1, outer):
+            line_copy(chunk, turn).wait_recv()
+            total = total + line_in[chunk, turn - 1]
+        out_ref[:, chunk * rows:(chunk + 1) * rows] = total
+    for chunk in range(chunks):
+        for hop in range(1, n_slab):
+            back_copy(chunk, hop).wait_send()
+        for turn in range(outer):
+            for hop in range(1, inner):
+                side_copy(chunk, hop, turn).wait_send()
+            if turn:
+                line_copy(chunk, turn).wait_send()
+
+
+def return_sum(ids, weights, solved, basis, depth_mat, turn_mat, n_orb, n_slab):
+    outer, inner = axis_parts(n_orb)
+    slots, grid_len, slab_len, width = solved.shape
+    couples_own = basis.shape[0] // n_orb
+    chunks = max(1, min(4, slab_len // 2))
+    planes = slab_len // chunks
+    rows = planes * grid_len
+    sides, lines = max(inner - 1, 1), max(outer - 1, 1)
+    dma, vmem, f32 = pltpu.SemaphoreType.DMA, pltpu.VMEM, jnp.float32
+    smem = pl.BlockSpec(memory_space=pltpu.SMEM)
+    block = (couples_own, rows, width)
+    return pl.pallas_call(
+        functools.partial(return_kernel, n_orb, n_slab, chunks, couples_own),
+        out_shape=jax.ShapeDtypeStruct((couples_own, slab_len * grid_len, width), f32),
+        in_specs=[smem, smem] + [VMEM_SPEC] * 4,
+        out_specs=VMEM_SPEC,
+        scratch_shapes=[
+            vmem((chunks, slots, planes, grid_len, width), f32),
+            vmem((2 * slots, rows, width), f32),
+            vmem((rows, width), f32),
+            vmem((chunks, n_orb) + block, f32),
+            vmem((chunks, sides, outer) + block, f32),
+            vmem((chunks, lines) + block, f32),
+            vmem((chunks, outer) + block, f32),
+            dma((chunks,)),
+            dma((chunks, max(n_slab - 1, 1))), dma((chunks, max(n_slab - 1, 1))),
+            dma((chunks, sides, outer)), dma((chunks, sides, outer)),
+            dma((chunks, lines)), dma((chunks, lines)),
+        ],
+        compiler_params=pltpu.CompilerParams(collective_id=1, has_side_effects=True),
+    )(ids, weights, solved, basis, depth_mat, turn_mat)
+
+
+def local(orbitals, pair_table, n_orb, n_slab):
     couples_own, slab_len, grid_len, width = orbitals.shape
     rows = slab_len * grid_len
     capacity = pair_table.shape[0]
@@ -382,20 +437,14 @@
         in_specs=[slot_spec, whole(kernel.shape), whole(turn_mat.shape)],
         out_specs=slot_spec,
     )(crossed.reshape(per_device, rows, width), kernel, turn_mat)
-    returned = lax.all_to_all(solved.reshape(per_device, grid_len, slab_len, width), "slab",
-                              split_axis=1, concat_axis=2, tiled=True)
-    totals = pl.pallas_call(
-        functools.partial(backward_kernel, grid_len),
-        out_shape=jax.ShapeDtypeStruct((couples, rows, width), jnp.float32),
-        grid_spec=pltpu.PrefetchScalarGridSpec(
-            num_scalar_prefetch=1, grid=(per_device,),
-            in_specs=[slot_spec, left_spec, right_spec, whole(depth_mat.shape),
-                      whole(turn_mat.shape)],
-            out_specs=whole((couples, rows, width)),
-            scratch_shapes=[pltpu.VMEM((rows, width), jnp.float32)]),
-    )(ids, returned.reshape(per_device, rows, width), gathered, gathered, depth_mat, turn_mat)
-
-    own = scatter_sum(totals.reshape(n_orb, couples_own * rows, width), n_orb)
+    couple_ids = jnp.arange(couples, dtype=jnp.int32)[:, None]
+    first_on = (couple_ids == ids[None, :, 0]) & (ids[None, :, 3] == 1)
+    second_on = (couple_ids == ids[None, :, 1]) & (ids[None, :, 3] == 1) & (
+        ids[None, :, 0] != ids[None, :, 1])
+    weights = jnp.stack([first_on, second_on], axis=2).reshape(couples, 2 * per_device)
+    own = return_sum(ids, weights.astype(jnp.float32),
+                     solved.reshape(per_device, grid_len, slab_len, width),
+                     gathered, depth_mat, turn_mat, n_orb, n_slab)
     own = own.reshape(couples_own, rows, width)
     cell_count = grid_len * grid_len * grid_len
 
@@ -419,6 +468,6 @@
 def solution(mesh):
     placed = (P("orb", "slab", None, None), P("orb", None))
     return jax.shard_map(
-        functools.partial(local, n_orb=mesh.shape["orb"]),
+        functools.partial(local, n_orb=mesh.shape["orb"], n_slab=mesh.shape["slab"]),
         mesh=mesh, in_specs=placed, out_specs=P("orb", "slab", None, None), check_vma=False
     )

time: 212 us -> 173 us (0.82)
  blocking collectives: 39.5 us -> 8.8 us
  Pallas kernels: 115 us -> 112 us
  local copies, waits for them, and re-layouts: 16.4 us -> 13.8 us
    all_to_all x1 -> x0, blocking collectives: 33.8 us -> none  [local(): lax.all_to_all(solved.reshape(per_device, grid_len, slab_len, width), 'sl...]
    pallas_call x2 -> x1, Pallas kernels: 69.7 us -> 66.5 us  [return_sum(): pl.pallas_call(functools.partial(return_kernel, n_orb, n_slab, chunks, co...]
    psum x1, blocking collectives: 5.74 us -> 8.8 us  [local(): both = lax.psum(lanes(jnp.stack([straight, across])) / cell_count, 'slab')]
where the time goes in v1:
time: 173 us
  Pallas kernels  112 us (65%)
  waiting for transfers between devices  29 us (17%)
  local copies, waits for them, and re-layouts  13.8 us (8%)
  blocking collectives  8.8 us (5%)
  other arithmetic  5.19 us (3%)
  starting transfers between devices  3.65 us (2%)
    pallas_call x1, Pallas kernels, return_sum(): pl.pallas_call(functools.partial(return_kernel, n_orb, n_slab, chunks, co...  66.5 us
    pallas_call x1, Pallas kernels, gather_all(): pl.pallas_call(functools.partial(gather_kernel, count), out_shape=(jax.Sh...  32.4 us
    all_to_all x1, waiting for transfers between devices, local(): lax.all_to_all(spectra.reshape(per_device, slab_len, grid_len, width), 's...  29 us
    psum x1, blocking collectives, local(): both = lax.psum(lanes(jnp.stack([straight, across])) / cell_count, 'slab')  8.8 us
    pallas_call x1, Pallas kernels, local(): pl.pallas_call(functools.partial(forward_kernel, grid_len), out_shape=slo...  7 us
    pallas_call x1, Pallas kernels, local(): pl.pallas_call(functools.partial(middle_kernel, grid_len, slab_len), out_...  6.22 us
    reshape x1, local copies, waits for them, and re-layouts, local(): spectra.reshape(per_device, slab_len, grid_len, width)  4.76 us
    all_to_all x1, starting transfers between devices, local(): lax.all_to_all(spectra.reshape(per_device, slab_len, grid_len, width), 's...  3.65 us
  transfers between devices with their start and end apart: 1, of which 1 were waited for; matrix products, arithmetic and copies ran while one was open for 1% of the time, Pallas kernels for 0%

profile of v1, /device:TPU:0, one launch (start us, length us, event | category | flops | bytes accessed | tf_op | source)
XLA Modules:
  0.0 172.6 jit_solution(1334662226058147477)
XLA Ops:
  0.0 0.8 copy.34
  0.8 0.6 pad.4.table_ref
  1.4 32.4 %shard_map.46 = (bf16[8,1024,128]{2,1,0:T(8,128)(2,1)}, s32[8,8,128]{2,1,0:T(8,128)}) custom-call(bf16[1024,128]{1,0:T(8,128)(2,1)} %bitcast.37, s32[8,128]{1,0:T(8,128)} %pad.4.table_ref), custom_call_target="tpu_custom_call" | custom-call | tf_op jit(solution)/shard_map/pallas_call | solution.py:174
  33.7 0.8 copy.47
  34.6 0.1 copy.36
  34.7 0.1 reduce-window.8
  34.8 0.1 add_reduce_fusion
  34.9 0.8 copy.37
  35.7 0.2 fusion.12
  35.9 0.1 copy.38
  36.0 0.2 select_reduce_fusion
  36.2 0.7 pad_add_fusion.ids_ref
  36.9 7.0 %shard_map.47 = f32[5,1024,128]{2,1,0:T(8,128)} custom-call(s32[5,4]{1,0:T(8,128)} %pad_add_fusion.ids_ref, bf16[8,1024,128]{2,1,0:T(8,128)(2,1)} %get-tuple-element.8.left_ref.right_ref.basis_ref, bf16[8,1024,128]{2,1,0:T(8,128)(2,1)} %get-tuple-element.8.left_ref.right_ref.basis_ref, bf16[256,256]{1,0:T(8,128)(2,1)} %constant.64.clone.depth_ref, ...), custom_call_target="tpu_custom_call" | custom-call | tf_op jit(solution)/shard_map/pallas_call | solution.py:423
  43.9 4.8 %copy.39 = f32[5,16,64,128]{3,1,0,2:T(8,128)} copy(f32[5,16,64,128]{3,2,1,0:T(8,128)} %bitcast.35) | data formatting | bytes 5242880 | tf_op jit(solution)/shard_map/reshape | solution.py:431
  48.6 3.7 %all-to-all-start = ((f32[5,16,64,128]{3,1,0,2:T(8,128)}), f32[5,16,64,128]{3,1,0,2:T(8,128)S(1)}, u32[]{:S(2)}, u32[]{:S(2)}) async-start(f32[5,16,64,128]{3,1,0,2:T(8,128)} %copy.39), calls=%async_computation | async-start | bytes 5242880 | tf_op jit(solution)/shard_map/all_to_all | solution.py:431
  52.3 0.2 slice_reduce_fusion
  52.5 0.1 compare_and_fusion
  52.6 0.7 copy.42.weights_ref
  53.3 0.1 add.83
  53.4 0.1 add.78
  53.5 0.1 add.79
  53.5 1.0 compare_select_fusion.kernel_ref
  54.6 29.0 %all-to-all-done = f32[5,16,64,128]{3,1,0,2:T(8,128)S(1)} async-done(((f32[5,16,64,128]{3,1,0,2:T(8,128)}), f32[5,16,64,128]{3,1,0,2:T(8,128)S(1)}, u32[]{:S(2)}, u32[]{:S(2)}) %all-to-all-start) | async-done | bytes 2621472 | tf_op jit(solution)/shard_map/all_to_all | solution.py:431
  83.5 2.5 %copy.41 = f32[5,4,16,16,128]{4,3,2,1,0:T(8,128)} copy(f32[5,4,16,16,128]{4,2,0,3,1:T(8,128)S(1)} %bitcast.32) | data formatting | bytes 5242880 | tf_op jit(solution)/shard_map/all_to_all | solution.py:431
  86.0 6.2 %shard_map.48 = f32[5,1024,128]{2,1,0:T(8,128)} custom-call(f32[5,1024,128]{2,1,0:T(8,128)} %bitcast.34, f32[1024,128]{1,0:T(8,128)} %compare_select_fusion.kernel_ref, bf16[64,192]{1,0:T(8,128)(2,1)} %constant.63.clone.turn_ref), custom_call_target="tpu_custom_call" | custom-call | tf_op jit(solution)/shard_map/pallas_call | solution.py:433
  92.2 66.5 %shard_map.49 = f32[1,1024,128]{2,1,0:T(8,128)} custom-call(s32[5,4]{1,0:T(8,128)} %pad_add_fusion.ids_ref, f32[8,10]{1,0:T(8,128)} %copy.42.weights_ref, f32[5,64,16,128]{3,2,1,0:T(8,128)} %bitcast.33, bf16[8,1024,128]{2,1,0:T(8,128)(2,1)} %get-tuple-element.8.left_ref.right_ref.basis_ref, bf16[256,256]{1,0:T(8,128)(2,1)} %constant.64.clone.depth_ref, ...), custom_call_target="tpu_custom_call" | custom-call | tf_op jit(solution)/shard_map/pallas_call | solution.py:365
  158.7 0.0 copy-start
  158.7 0.0 copy-start.1
  158.7 1.6 fusion.14
  160.3 0.2 maximum_bitcast_fusion
  160.5 0.1 copy-done
  160.6 0.1 copy-done.1
  160.7 0.7 fusion
  161.4 0.1 stack.15
  161.5 0.1 stack.16
  161.5 0.1 maximum_reduce_fusion
  161.6 0.1 broadcast_in_dim.31
  161.7 0.1 div.19
  161.8 8.8 %psum.7 = f32[2,1,8,128]{3,2,1,0:T(8,128)S(1)} all-reduce(f32[2,1,8,128]{3,2,1,0:T(8,128)S(1)} %div.19), channel_id=1, replica_groups=mesh['orb'=8,'slab'=4] {'slab'}, use_global_device_ids=true, to_apply=%region_6.7 | all-reduce | flops 2048 | bytes 16384 | tf_op jit(solution)/shard_map/psum | solution.py:462
  170.6 0.7 fusion.2
  171.4 0.2 fusion.13
  171.6 1.0 maximum_subtract_fusion
  (13 shorter events, 0.1 us)
Async XLA Ops:
  48.6 34.9 %all-to-all-start = ((f32[5,16,64,128]{3,1,0,2:T(8,128)}), f32[5,16,64,128]{3,1,0,2:T(8,128)S(1)}, u32[]{:S(2)}, u32[]{:S(2)}) async-start(f32[5,16,64,128]{3,1,0,2:T(8,128)} %copy.39), calls=%async_computation | async-start | bytes 5242880 | tf_op jit(solution)/shard_map/all_to_all | solution.py:431
  158.7 1.9 %copy-start = (bf16[8,1024,128]{2,1,0:T(8,128)(2,1)S(1)}, bf16[8,1024,128]{2,1,0:T(8,128)(2,1)}, u32[]{:S(2)}) copy-start(bf16[8,1024,128]{2,1,0:T(8,128)(2,1)} %get-tuple-element.8.left_ref.right_ref.basis_ref) | copy-start | bytes 6291460
  158.7 2.0 %copy-start.1 = (f32[1,1024,128]{2,1,0:T(8,128)S(1)}, f32[1,1024,128]{2,1,0:T(8,128)}, u32[]{:S(2)}) copy-start(f32[1,1024,128]{2,1,0:T(8,128)} %shard_map.49) | copy-start | bytes 1572868

commit v2 on v1

--- a/solution.py
+++ b/solution.py
@@ -71,119 +71,35 @@
     pl.semaphore_wait(barrier, count - 1)
 
 
-def gather_kernel(count, own_ref, table_ref, out_ref, tables_ref, local_sem, up_send, up_recv,
-                  down_send, down_recv, side_send, side_recv, tab_send, tab_recv):
-    outer, inner = axis_parts(count)
+def table_kernel(count, table_ref, tables_ref, send_sem, recv_sem):
     me = lax.axis_index("orb")
-    z_pos, x_pos = me // inner, me % inner
     greet_all(count, me)
 
-    def slot(z_at, x_at):
-        return out_ref.at[z_at * inner + x_at]
-
-    def up_copy(step, src):
-        return pltpu.make_async_remote_copy(
-            src_ref=src, dst_ref=slot(z_pos - step, x_pos), send_sem=up_send.at[step],
-            recv_sem=up_recv.at[step], device_id=peer((z_pos + 1) * inner + x_pos),
+    def tab_copy(step):
+        return pltpu.make_async_remote_copy(
+            src_ref=table_ref, dst_ref=tables_ref.at[me], send_sem=send_sem.at[step - 1],
+            recv_sem=recv_sem.at[step - 1], device_id=peer(lax.rem(me + step, count)),
             device_id_type=MESH)
 
-    def down_copy(step, src):
-        return pltpu.make_async_remote_copy(
-            src_ref=src, dst_ref=slot(z_pos + step, x_pos), send_sem=down_send.at[step],
-            recv_sem=down_recv.at[step], device_id=peer((z_pos - 1) * inner + x_pos),
-            device_id_type=MESH)
-
-    def side_copy(hop, z_at, src):
-        return pltpu.make_async_remote_copy(
-            src_ref=src, dst_ref=slot(z_at, x_pos), send_sem=side_send.at[hop - 1, z_at],
-            recv_sem=side_recv.at[hop - 1, z_at],
-            device_id=peer(z_pos * inner + lax.rem(x_pos + hop, inner)), device_id_type=MESH)
-
-    def tab_copy(step):
-        return pltpu.make_async_remote_copy(
-            src_ref=table_ref, dst_ref=tables_ref.at[me], send_sem=tab_send.at[step - 1],
-            recv_sem=tab_recv.at[step - 1], device_id=peer(lax.rem(me + step, count)),
-            device_id_type=MESH)
-
-    has_up, has_down = z_pos + 1 < outer, z_pos >= 1
-
-    @pl.when(has_up)
-    def _():
-        up_copy(0, own_ref).start()
-
-    @pl.when(has_down)
-    def _():
-        down_copy(0, own_ref).start()
-
-    for hop in range(1, inner):
-        side_copy(hop, z_pos, own_ref).start()
     for step in range(1, count):
         tab_copy(step).start()
-    keep = pltpu.make_async_copy(own_ref, out_ref.at[me], local_sem.at[0])
-    keep.start()
-    keep_tab = pltpu.make_async_copy(table_ref, tables_ref.at[me], local_sem.at[1])
-    keep_tab.start()
-
-    for step in range(1, outer):
-        @pl.when(z_pos - step >= 0)
-        def _():
-            held = slot(z_pos - step, x_pos)
-            up_copy(step - 1, held).wait_recv()
-
-            @pl.when(has_up)
-            def _():
-                up_copy(step, held).start()
-
-            for hop in range(1, inner):
-                side_copy(hop, z_pos - step, held).start()
-
-        @pl.when(z_pos + step < outer)
-        def _():
-            held = slot(z_pos + step, x_pos)
-            down_copy(step - 1, held).wait_recv()
-
-            @pl.when(has_down)
-            def _():
-                down_copy(step, held).start()
-
-            for hop in range(1, inner):
-                side_copy(hop, z_pos + step, held).start()
-
-    keep.wait()
-    keep_tab.wait()
-    for hop in range(1, inner):
-        for z_at in range(outer):
-            side_copy(hop, z_at, own_ref).wait_recv()
-            side_copy(hop, z_at, own_ref).wait_send()
+    tables_ref[me] = table_ref[...]
     for step in range(1, count):
         tab_copy(step).wait_recv()
+    for step in range(1, count):
         tab_copy(step).wait_send()
-    for step in range(outer):
-        @pl.when(has_up & (z_pos - step >= 0))
-        def _():
-            up_copy(step, own_ref).wait_send()
-
-        @pl.when(has_down & (z_pos + step < outer))
-        def _():
-            down_copy(step, own_ref).wait_send()
-
-
-def gather_all(own, table, count):
-    outer, inner = axis_parts(count)
+
+
+def gather_tables(table, count):
     dma = pltpu.SemaphoreType.DMA
     return pl.pallas_call(
-        functools.partial(gather_kernel, count),
-        out_shape=(
-            jax.ShapeDtypeStruct((count,) + own.shape, own.dtype),
-            jax.ShapeDtypeStruct((count,) + table.shape, table.dtype),
-        ),
-        in_specs=[VMEM_SPEC, VMEM_SPEC],
-        out_specs=(ANY_SPEC, ANY_SPEC),
-        scratch_shapes=[dma((2,)), dma((outer,)), dma((outer,)), dma((outer,)), dma((outer,)),
-                        dma((max(inner - 1, 1), outer)), dma((max(inner - 1, 1), outer)),
-                        dma((count - 1,)), dma((count - 1,))],
+        functools.partial(table_kernel, count),
+        out_shape=jax.ShapeDtypeStruct((count,) + table.shape, table.dtype),
+        in_specs=[VMEM_SPEC],
+        out_specs=VMEM_SPEC,
+        scratch_shapes=[dma((count - 1,)), dma((count - 1,))],
         compiler_params=pltpu.CompilerParams(collective_id=0, has_side_effects=True),
-    )(own, table)
+    )(table)
 
 
 def depth_turn(rows, depth_ref):
@@ -200,19 +116,193 @@
                    preferred_element_type=jnp.float32)
 
 
-def forward_kernel(grid_len, ids_ref, left_ref, right_ref, depth_ref, turn_ref, out_ref):
-    step = pl.program_id(0)
-    left = left_ref[0].astype(jnp.float32)
-    right = right_ref[0].astype(jnp.float32)
-    width = right.shape[1]
-    partner = jnp.where(ids_ref[step, 2] == 1, pltpu.roll(right, grid_len, 1), right)
-    density = jnp.where(ids_ref[step, 3] == 1, left * partner, 0.0)
-    flat = depth_turn(density, depth_ref)
-    for x_at in range(0, flat.shape[0] // grid_len, 2):
-        low, mid, high = x_at * grid_len, (x_at + 1) * grid_len, (x_at + 2) * grid_len
-        done = pair_turn(flat[low:mid], flat[mid:high], turn_ref)
-        out_ref[0, low:mid] = done[:, :width]
-        out_ref[0, mid:high] = done[:, width:]
+def greet_both(n_orb, n_slab, me, me_slab):
+    barrier = pltpu.get_barrier_semaphore()
+    for step in range(1, n_orb):
+        pl.semaphore_signal(barrier, inc=1, device_id=peer(lax.rem(me + step, n_orb)),
+                            device_id_type=MESH)
+    for step in range(1, n_slab):
+        pl.semaphore_signal(barrier, inc=1, device_id={"slab": lax.rem(me_slab + step, n_slab)},
+                            device_id_type=MESH)
+    pl.semaphore_wait(barrier, n_orb + n_slab - 2)
+
+
+def chunk_count(slab_len):
+    return max(1, min(4, slab_len // 2))
+
+
+def advance_kernel(n_orb, n_slab, chunks, grid_len, ids_ref, own_ref, depth_ref, turn_ref,
+                   basis_ref, out_ref, *scratch):
+    held = scratch[:chunks]
+    (spectra, keep_sem, stay_sem, up_send, up_recv, down_send, down_recv, side_send, side_recv,
+     cross_send, cross_recv) = scratch[chunks:]
+    outer, inner = axis_parts(n_orb)
+    me, me_slab = lax.axis_index("orb"), lax.axis_index("slab")
+    z_pos, x_pos = me // inner, me % inner
+    couples_own = own_ref.shape[0]
+    slots, _, slab_len, width = out_ref.shape
+    planes = slab_len // chunks
+    rows = planes * grid_len
+    greet_both(n_orb, n_slab, me, me_slab)
+
+    def mine(chunk):
+        return own_ref.at[:, pl.ds(chunk * rows, rows)]
+
+    def place(chunk, z_at):
+        return held[chunk].at[pl.ds((z_at * inner + x_pos) * couples_own, couples_own)]
+
+    def up_copy(chunk, step, src):
+        return pltpu.make_async_remote_copy(
+            src_ref=src, dst_ref=place(chunk, z_pos - step), send_sem=up_send.at[chunk, step],
+            recv_sem=up_recv.at[chunk, step], device_id=peer((z_pos + 1) * inner + x_pos),
+            device_id_type=MESH)
+
+    def down_copy(chunk, step, src):
+        return pltpu.make_async_remote_copy(
+            src_ref=src, dst_ref=place(chunk, z_pos + step), send_sem=down_send.at[chunk, step],
+            recv_sem=down_recv.at[chunk, step], device_id=peer((z_pos - 1) * inner + x_pos),
+            device_id_type=MESH)
+
+    def side_copy(chunk, hop, z_at, src):
+        return pltpu.make_async_remote_copy(
+            src_ref=src, dst_ref=place(chunk, z_at), send_sem=side_send.at[chunk, hop - 1, z_at],
+            recv_sem=side_recv.at[chunk, hop - 1, z_at],
+            device_id=peer(z_pos * inner + lax.rem(x_pos + hop, inner)), device_id_type=MESH)
+
+    def keep_copy(chunk):
+        return pltpu.make_async_copy(mine(chunk), place(chunk, z_pos), keep_sem.at[chunk])
+
+    def cross_copy(chunk, hop):
+        to = lax.rem(me_slab + hop, n_slab)
+        return pltpu.make_async_remote_copy(
+            src_ref=spectra.at[chunk, :, :,
+                               pl.ds(pl.multiple_of(to * slab_len, slab_len), slab_len)],
+            dst_ref=out_ref.at[:, pl.ds(me_slab * slab_len + chunk * planes, planes)],
+            send_sem=cross_send.at[chunk, hop - 1], recv_sem=cross_recv.at[chunk, hop - 1],
+            device_id={"slab": to}, device_id_type=MESH)
+
+    def stay_copy(chunk):
+        return pltpu.make_async_copy(
+            spectra.at[chunk, :, :,
+                       pl.ds(pl.multiple_of(me_slab * slab_len, slab_len), slab_len)],
+            out_ref.at[:, pl.ds(me_slab * slab_len + chunk * planes, planes)],
+            stay_sem.at[chunk])
+
+    has_up, has_down = z_pos + 1 < outer, z_pos >= 1
+
+    for chunk in range(chunks):
+        @pl.when(has_up)
+        def _():
+            up_copy(chunk, 0, mine(chunk)).start()
+
+        @pl.when(has_down)
+        def _():
+            down_copy(chunk, 0, mine(chunk)).start()
+
+        for hop in range(1, inner):
+            side_copy(chunk, hop, z_pos, mine(chunk)).start()
+        keep_copy(chunk).start()
+
+    def relay(chunk, step):
+        @pl.when(z_pos - step >= 0)
+        def _():
+            got = place(chunk, z_pos - step)
+            up_copy(chunk, step - 1, got).wait_recv()
+
+            @pl.when(has_up)
+            def _():
+                up_copy(chunk, step, got).start()
+
+            for hop in range(1, inner):
+                side_copy(chunk, hop, z_pos - step, got).start()
+
+        @pl.when(z_pos + step < outer)
+        def _():
+            got = place(chunk, z_pos + step)
+            down_copy(chunk, step - 1, got).wait_recv()
+
+            @pl.when(has_down)
+            def _():
+                down_copy(chunk, step, got).start()
+
+            for hop in range(1, inner):
+                side_copy(chunk, hop, z_pos + step, got).start()
+
+    def compute(chunk):
+        keep_copy(chunk).wait()
+        for hop in range(1, inner):
+            for z_at in range(outer):
+                side_copy(chunk, hop, z_at, mine(chunk)).wait_recv()
+
+        @pl.loop(0, slots)
+        def _(slot):
+            left = held[chunk][ids_ref[slot, 0]].astype(jnp.float32)
+            right = held[chunk][ids_ref[slot, 1]].astype(jnp.float32)
+            flipped = ids_ref[slot, 2] == 1
+            partner = jnp.where(flipped, pltpu.roll(right, grid_len, 1), right)
+            density = jnp.where(ids_ref[slot, 3] == 1, left * partner, 0.0)
+            flat = depth_turn(density, depth_ref)
+            for x_at in range(0, planes, 2):
+                low, mid, high = x_at * grid_len, (x_at + 1) * grid_len, (x_at + 2) * grid_len
+                done = pair_turn(flat[low:mid], flat[mid:high], turn_ref)
+                spectra[chunk, slot, x_at] = done[:, :width]
+                spectra[chunk, slot, x_at + 1] = done[:, width:]
+
+        for hop in range(1, n_slab):
+            cross_copy(chunk, hop).start()
+        stay_copy(chunk).start()
+        basis_ref[:, chunk * rows:(chunk + 1) * rows] = held[chunk][...]
+
+    for wave in range(1, chunks + outer - 1):
+        for step in range(outer - 1, 0, -1):
+            if 0 <= wave - step < chunks:
+                relay(wave - step, step)
+        if wave - (outer - 1) >= 0:
+            compute(wave - (outer - 1))
+
+    for chunk in range(chunks):
+        stay_copy(chunk).wait()
+        for hop in range(1, n_slab):
+            cross_copy(chunk, hop).wait_recv()
+            cross_copy(chunk, hop).wait_send()
+        for hop in range(1, inner):
+            for z_at in range(outer):
+                side_copy(chunk, hop, z_at, mine(chunk)).wait_send()
+        for step in range(outer):
+            @pl.when(has_up & (z_pos - step >= 0))
+            def _():
+                up_copy(chunk, step, mine(chunk)).wait_send()
+
+            @pl.when(has_down & (z_pos + step < outer))
+            def _():
+                down_copy(chunk, step, mine(chunk)).wait_send()
+
+
+def advance(ids, own, depth_mat, turn_mat, grid_len, n_orb, n_slab):
+    outer, inner = axis_parts(n_orb)
+    slots = ids.shape[0]
+    couples_own, all_rows, width = own.shape
+    slab_len = all_rows // grid_len
+    chunks = chunk_count(slab_len)
+    planes = slab_len // chunks
+    rows = planes * grid_len
+    sides, slabs = max(inner - 1, 1), max(n_slab - 1, 1)
+    dma, vmem, f32 = pltpu.SemaphoreType.DMA, pltpu.VMEM, jnp.float32
+    return pl.pallas_call(
+        functools.partial(advance_kernel, n_orb, n_slab, chunks, grid_len),
+        out_shape=(jax.ShapeDtypeStruct((n_orb * couples_own, all_rows, width), own.dtype),
+                   jax.ShapeDtypeStruct((slots, grid_len, slab_len, width), f32)),
+        in_specs=[pl.BlockSpec(memory_space=pltpu.SMEM)] + [VMEM_SPEC] * 3,
+        out_specs=(VMEM_SPEC, VMEM_SPEC),
+        scratch_shapes=[vmem((n_orb * couples_own, rows, width), own.dtype)] * chunks + [
+            vmem((chunks, slots, planes, grid_len, width), f32),
+            dma((chunks,)), dma((chunks,)),
+            dma((chunks, outer)), dma((chunks, outer)), dma((chunks, outer)), dma((chunks, outer)),
+            dma((chunks, sides, outer)), dma((chunks, sides, outer)),
+            dma((chunks, slabs)), dma((chunks, slabs)),
+        ],
+        compiler_params=pltpu.CompilerParams(collective_id=2, has_side_effects=True),
+    )(ids, own, depth_mat, turn_mat)
 
 
 def middle_kernel(grid_len, slab_len, in_ref, kernel_ref, turn_ref, out_ref):
@@ -237,15 +327,7 @@
     planes = slab_len // chunks
     rows = planes * grid_len
 
-    barrier = pltpu.get_barrier_semaphore()
-    for step in range(1, n_orb):
-        pl.semaphore_signal(barrier, inc=1, device_id=peer(lax.rem(me + step, n_orb)),
-                            device_id_type=MESH)
-    for step in range(1, n_slab):
-        pl.semaphore_signal(barrier, inc=1, device_id={"slab": lax.rem(me_slab + step, n_slab)},
-                            device_id_type=MESH)
-    pl.semaphore_wait(barrier, n_orb + n_slab - 2)
-
+    greet_both(n_orb, n_slab, me, me_slab)
     own_rows = pl.ds(pl.multiple_of(me_slab * slab_len, slab_len), slab_len)
 
     def back_copy(chunk, hop):
@@ -355,7 +437,7 @@
     outer, inner = axis_parts(n_orb)
     slots, grid_len, slab_len, width = solved.shape
     couples_own = basis.shape[0] // n_orb
-    chunks = max(1, min(4, slab_len // 2))
+    chunks = chunk_count(slab_len)
     planes = slab_len // chunks
     rows = planes * grid_len
     sides, lines = max(inner - 1, 1), max(outer - 1, 1)
@@ -390,8 +472,7 @@
     capacity = pair_table.shape[0]
     couples = couples_own * n_orb
     padded = jnp.pad(pair_table, ((0, 0), (0, 128 - pair_table.shape[1])), constant_values=-1)
-    gathered, tables = gather_all(orbitals.reshape(couples_own * rows, width), padded, n_orb)
-    gathered = gathered.reshape(couples, rows, width)
+    tables = gather_tables(padded, n_orb)
     table = tables.reshape(n_orb * capacity, 128)[:, :3]
 
     live_total = sum(capacity * (k + 1) // n_orb for k in range(n_orb))
@@ -415,21 +496,11 @@
     def whole(shape):
         return pl.BlockSpec(shape, lambda j, *ids: (0,) * len(shape))
 
-    left_spec = pl.BlockSpec((1, rows, width), lambda j, ids: (ids[j, 0], 0, 0))
-    right_spec = pl.BlockSpec((1, rows, width), lambda j, ids: (ids[j, 1], 0, 0))
     slot_spec = pl.BlockSpec((1, rows, width), lambda j, *ids: (j, 0, 0))
     slots_shape = jax.ShapeDtypeStruct((per_device, rows, width), jnp.float32)
 
-    spectra = pl.pallas_call(
-        functools.partial(forward_kernel, grid_len),
-        out_shape=slots_shape,
-        grid_spec=pltpu.PrefetchScalarGridSpec(
-            num_scalar_prefetch=1, grid=(per_device,),
-            in_specs=[left_spec, right_spec, whole(depth_mat.shape), whole(turn_mat.shape)],
-            out_specs=slot_spec),
-    )(ids, gathered, gathered, depth_mat, turn_mat)
-    crossed = lax.all_to_all(spectra.reshape(per_device, slab_len, grid_len, width), "slab",
-                             split_axis=2, concat_axis=1, tiled=True)
+    gathered, crossed = advance(ids, orbitals.reshape(couples_own, rows, width), depth_mat,
+                                turn_mat, grid_len, n_orb, n_slab)
     solved = pl.pallas_call(
         functools.partial(middle_kernel, grid_len, slab_len),
         out_shape=slots_shape,

time: 173 us -> 155 us (0.90)
  waiting for transfers between devices: 29 us -> 0 us
  Pallas kernels: 112 us -> 134 us
  local copies, waits for them, and re-layouts: 13.8 us -> 6.58 us
  starting transfers between devices: 3.65 us -> 0 us
    all_to_all x1 -> x0, waiting for transfers between devices: 29 us -> none  [local(): lax.all_to_all(spectra.reshape(per_device, slab_len, grid_len, width), 's...]
    pallas_call x2, Pallas kernels: 39.4 us -> 61.5 us  [the longest x1 51.7 us: advance(): pl.pallas_call(functools.partial(advance_kernel, n_orb, n_slab, chunks, g...]
    reshape x1 -> x0, local copies, waits for them, and re-layouts: 4.76 us -> none  [local(): spectra.reshape(per_device, slab_len, grid_len, width)]
    all_to_all x1 -> x0, starting transfers between devices: 3.65 us -> none  [local(): lax.all_to_all(spectra.reshape(per_device, slab_len, grid_len, width), 's...]
    all_to_all x1 -> x0, local copies, waits for them, and re-layouts: 2.46 us -> none  [local(): lax.all_to_all(spectra.reshape(per_device, slab_len, grid_len, width), 's...]
  transfers between devices with their start and end apart: 1 -> 0, of which waited for: 1 -> 0; matrix products, arithmetic and copies ran while one was open for 1% -> 0% of each run, Pallas kernels for 0% -> 0%
where the time goes in v2:
time: 155 us; the launch traced here: 154 us
  Pallas kernels  134 us (86%)
  blocking collectives  8.01 us (5%)
  local copies, waits for them, and re-layouts  6.58 us (4%)
  other arithmetic  5.19 us (3%)
    pallas_call x1, Pallas kernels, return_sum(): pl.pallas_call(functools.partial(return_kernel, n_orb, n_slab, chunks, co...  66.6 us
    pallas_call x1, Pallas kernels, advance(): pl.pallas_call(functools.partial(advance_kernel, n_orb, n_slab, chunks, g...  51.7 us
    pallas_call x1, Pallas kernels, gather_tables(): pl.pallas_call(functools.partial(table_kernel, count), out_shape=jax.Shap...  9.75 us
    psum x1, blocking collectives, local(): both = lax.psum(lanes(jnp.stack([straight, across])) / cell_count, 'slab')  8.01 us
    pallas_call x1, Pallas kernels, local(): pl.pallas_call(functools.partial(middle_kernel, grid_len, slab_len), out_...  6.24 us

profile of v2, /device:TPU:0, one launch (start us, length us, event | category | flops | bytes accessed | tf_op | source)
XLA Modules:
  0.0 154.2 jit_solution(10024273874762983787)
XLA Ops:
  0.0 0.8 copy.22
  0.8 0.6 pad.4.table_ref
  1.4 9.8 %shard_map.46 = s32[8,8,128]{2,1,0:T(8,128)} custom-call(s32[8,128]{1,0:T(8,128)} %pad.4.table_ref), custom_call_target="tpu_custom_call" | custom-call | tf_op jit(solution)/shard_map/pallas_call | solution.py:95
  11.2 0.8 copy.31
  12.0 0.8 copy.25
  12.8 0.1 copy.24
  12.9 0.1 reduce-window.8
  13.0 0.1 add_reduce_fusion
  13.1 0.2 fusion.12
  13.3 0.2 select_reduce_fusion
  13.5 0.2 slice_reduce_fusion
  13.7 0.1 compare_and_fusion
  13.9 0.7 copy.27.weights_ref
  14.5 0.1 copy.26
  14.6 0.7 pad_add_fusion.ids_ref
  15.3 0.1 add.78
  15.4 0.1 add.79
  15.4 0.1 add.83
  15.5 1.0 compare_select_fusion.kernel_ref
  16.5 51.7 %shard_map.47 = (bf16[8,1024,128]{2,1,0:T(8,128)(2,1)}, f32[5,64,16,128]{3,2,1,0:T(8,128)}) custom-call(s32[5,4]{1,0:T(8,128)} %pad_add_fusion.ids_ref, bf16[1,1024,128]{2,1,0:T(8,128)(2,1)} %bitcast.33, bf16[256,256]{1,0:T(8,128)(2,1)} %constant.64.clone.depth_ref, bf16[64,192]{1,0:T(8,128)(2,1)} %constant.63.clone.turn_ref), custom_call_target="tpu_custom_call" | custom-call | tf_op jit(solution)/shard_map/pallas_call | solution.py:291
  68.3 6.2 %shard_map.48 = f32[5,1024,128]{2,1,0:T(8,128)} custom-call(f32[5,1024,128]{2,1,0:T(8,128)} %bitcast.30, f32[1024,128]{1,0:T(8,128)} %compare_select_fusion.kernel_ref, bf16[64,192]{1,0:T(8,128)(2,1)} %constant.63.clone.turn_ref), custom_call_target="tpu_custom_call" | custom-call | tf_op jit(solution)/shard_map/pallas_call | solution.py:504
  74.5 66.6 %shard_map.49 = f32[1,1024,128]{2,1,0:T(8,128)} custom-call(s32[5,4]{1,0:T(8,128)} %pad_add_fusion.ids_ref, f32[8,10]{1,0:T(8,128)} %copy.27.weights_ref, f32[5,64,16,128]{3,2,1,0:T(8,128)} %bitcast.28, bf16[8,1024,128]{2,1,0:T(8,128)(2,1)} %get-tuple-element.8.basis_ref, bf16[256,256]{1,0:T(8,128)(2,1)} %constant.64.clone.depth_ref, ...), custom_call_target="tpu_custom_call" | custom-call | tf_op jit(solution)/shard_map/pallas_call | solution.py:447
  141.1 0.0 copy-start
  141.1 0.0 copy-start.1
  141.1 1.6 %fusion.14 = (f32[1,1024,64]{2,1,0:T(8,128)S(1)}, f32[1,1024,64]{2,1,0:T(8,128)S(1)}) fusion(f32[1,1024,128]{2,1,0:T(8,128)} %shard_map.49), kind=kLoop, calls=%fused_computation.45 | loop fusion | bytes 1048576 | tf_op jit(solution)/shard_map/slice | solution.py:523
  142.7 0.2 maximum_bitcast_fusion
  142.9 0.1 copy-done
  143.0 0.1 copy-done.1
  143.1 0.7 fusion
  143.8 0.1 stack.15
  143.9 0.1 stack.16
  144.0 0.1 maximum_reduce_fusion
  144.1 0.1 broadcast_in_dim.31
  144.1 0.1 div.19
  144.2 8.0 %psum.7 = f32[2,1,8,128]{3,2,1,0:T(8,128)S(1)} all-reduce(f32[2,1,8,128]{3,2,1,0:T(8,128)S(1)} %div.19), channel_id=1, replica_groups=mesh['orb'=8,'slab'=4] {'slab'}, use_global_device_ids=true, to_apply=%region_6.7 | all-reduce | flops 2048 | bytes 16384 | tf_op jit(solution)/shard_map/psum | solution.py:533
  152.3 0.7 fusion.2
  153.0 0.2 fusion.13
  153.2 1.0 maximum_subtract_fusion
  (13 shorter events, 0.1 us)
Async XLA Ops:
  141.1 1.9 %copy-start = (bf16[8,1024,128]{2,1,0:T(8,128)(2,1)S(1)}, bf16[8,1024,128]{2,1,0:T(8,128)(2,1)}, u32[]{:S(2)}) copy-start(bf16[8,1024,128]{2,1,0:T(8,128)(2,1)} %get-tuple-element.8.basis_ref) | copy-start | bytes 6291460
  141.1 2.0 %copy-start.1 = (f32[1,1024,128]{2,1,0:T(8,128)S(1)}, f32[1,1024,128]{2,1,0:T(8,128)}, u32[]{:S(2)}) copy-start(f32[1,1024,128]{2,1,0:T(8,128)} %shard_map.49) | copy-start | bytes 1572868
